TPU v7x, 256 devices: a whole 4x4x8 slice. The times are simulated.
256 devices in a mesh: front: 4 (over y), pivot: 8 (over x, core), rows: 8 (over z).
Axes of the slice: x: 4, y: 4, z: 8, core: 2. Of those that a mesh axis runs over, the one named last changes fastest.
Arguments:
- factor: float32 [4, 8, 1024, 8192], P('front', 'pivot', 'rows'), may hold values from -0.0625 to 0.0625
- inv_diag: float32 [4, 8, 1024, 1024], P('front', 'pivot', 'rows'), may hold values from -0.1875 to 0.1875
- boundary: float32 [4, 8192, 8192], P('front', ('pivot', 'rows')), may hold values from -0.0625 to 0.0625
- rhs: float32 [4, 240, 8192], P('front', None, ('pivot', 'rows')), may hold values from -6 to 6
- boundary_rhs: float32 [4, 240, 8192], P('front', None, ('pivot', 'rows')), may hold values from -6 to 6
- owner: int32 [4, 8192, 1], P('front', ('pivot', 'rows')), may hold values from 0 to 63; in each aligned block of 128 rows (0 to 127, 128 to 255, ..., all dimensions but the last counted through in order) at most 4 rows name the same one
- slot: int32 [4, 8192], P('front', ('pivot', 'rows')), may hold values from 0 to 255
- parent_in: float32 [240, 16384], P(None, ('pivot', 'rows')), may hold values from -6 to 6
Outputs:
- solution: float32 [4, 240, 8192], P('front', None, ('pivot', 'rows'))
- parent_rhs: float32 [240, 16384], P(None, ('pivot', 'rows'))
Inputs may be any that keep to these rules, and one draw needn't show every extreme that they name: Within the 128 boundary rows of one device no owner is named more than 4 times, and in every draw some device's rows name some owner exactly 4 times.
All inputs are finite; a program needn't handle non-finite values.
Results may differ from a plain program's by a relative error of at most 0.0001.
Values sent between devices are 32-bit elements; how exact they have to be, the bound alone decides.
A program may use at most 64 MiB of HBM per device.

v0:
```python
import jax
import jax.numpy as jnp
from jax import lax
from jax.sharding import PartitionSpec as P

highest = lax.Precision.HIGHEST


def shards(factor, inv_diag, boundary, rhs, boundary_rhs, owner, slot, parent_in):
    factor_rows = factor[0, 0]
    inv_rows = inv_diag[0, 0]
    bound_rows = boundary[0]
    local_rhs = rhs[0]
    local_brhs = boundary_rhs[0]
    block_count = lax.axis_size("pivot")
    row_count = lax.axis_size("rows")
    block_span = inv_rows.shape[1]
    slice_rows = factor_rows.shape[0]
    sources = local_rhs.shape[0]
    own_block = lax.axis_index("pivot")
    own_row = lax.axis_index("rows")
    contract = (((1,), (1,)), ((), ()))

    def solve_section(section_idx, carry):
        running, boundary_sum, own_solved = carry
        residual = local_rhs - running
        partial_value = jnp.dot(
            residual, inv_rows, precision=highest, preferred_element_type=jnp.float32
        )
        masked = jnp.where(own_block == section_idx, partial_value, 0.0)
        solved = lax.psum(masked, ("pivot", "rows"))
        pivot_tile = lax.dynamic_slice_in_dim(factor_rows, section_idx * block_span, block_span, 1)
        update_term = lax.dot_general(
            solved, pivot_tile, contract, precision=highest, preferred_element_type=jnp.float32
        )
        running = running + jnp.where(section_idx < own_block, update_term, 0.0)
        bound_tile = lax.dynamic_slice_in_dim(bound_rows, section_idx * block_span, block_span, 1)
        boundary_sum = boundary_sum + lax.dot_general(
            solved, bound_tile, contract, precision=highest, preferred_element_type=jnp.float32
        )
        own_piece = lax.dynamic_slice_in_dim(solved, own_row * slice_rows, slice_rows, 1)
        own_solved = jnp.where(own_block == section_idx, own_piece, own_solved)
        return (running, boundary_sum, own_solved)

    start = (
        jnp.zeros((sources, slice_rows), jnp.float32),
        jnp.zeros((sources, bound_rows.shape[0]), jnp.float32),
        jnp.zeros((sources, slice_rows), jnp.float32),
    )
    running, boundary_sum, own_solved = lax.fori_loop(0, block_count, solve_section, start)
    update = local_brhs - boundary_sum
    out_rows = update.T
    owners = owner[0, :, 0]
    slot_ids = slot[0]
    owner_count = block_count * row_count
    capacity = max(2, 2 * out_rows.shape[0] // owner_count)
    onehot = (owners[:, None] == jnp.arange(owner_count, dtype=jnp.int32)[None, :]).astype(
        jnp.int32
    )
    before = jnp.cumsum(onehot, axis=0) - onehot
    position = jnp.sum(before * onehot, axis=1)
    dest_slot = owners * capacity + position
    select = dest_slot[None, :] == jnp.arange(owner_count * capacity, dtype=jnp.int32)[:, None]
    send_rows = jnp.dot(
        select.astype(jnp.float32), out_rows, precision=highest, preferred_element_type=jnp.float32
    )
    send_slot = jnp.max(jnp.where(select, slot_ids[None, :], -1), axis=1)
    got_rows, got_slots = (
        lax.all_to_all(
            send_rows.reshape(owner_count, capacity, sources),
            ("pivot", "rows"),
            split_axis=0,
            concat_axis=0,
            tiled=True,
        ),
        lax.all_to_all(
            send_slot.reshape(owner_count, capacity),
            ("pivot", "rows"),
            split_axis=0,
            concat_axis=0,
            tiled=True,
        ),
    )
    got_rows = got_rows.reshape(owner_count * capacity, sources)
    got_slots = got_slots.reshape(owner_count * capacity)
    parent_rows = parent_in.shape[1]
    slot_hits = (got_slots[:, None] == jnp.arange(parent_rows, dtype=jnp.int32)[None, :]).astype(
        jnp.float32
    )
    local_part = jnp.einsum(
        "ks,ko->so", got_rows, slot_hits, precision=highest, preferred_element_type=jnp.float32
    )
    sibling_total = lax.psum(local_part, "front")
    parent = parent_in + sibling_total
    return (own_solved[None], parent)


def solution(mesh):
    placed = (
        P("front", "pivot", "rows", None),
        P("front", "pivot", "rows", None),
        P("front", ("pivot", "rows"), None),
        P("front", None, ("pivot", "rows")),
        P("front", None, ("pivot", "rows")),
        P("front", ("pivot", "rows"), None),
        P("front", ("pivot", "rows")),
        P(None, ("pivot", "rows")),
    )
    return jax.shard_map(
        shards,
        mesh=mesh,
        in_specs=placed,
        out_specs=(P("front", None, ("pivot", "rows")), P(None, ("pivot", "rows"))),
        check_vma=False,
    )
```

profile of v0, /device:TPU:2, one launch (start us, length us, event | category | flops | bytes accessed | tf_op | source)
XLA Modules:
  0.0 1667.7 jit_solution(10472206007967670768)
XLA Ops:
  11.9 12.0 all-to-all-start.1
  24.0 1568.2 %while.20 = (s32[]{:T(128)}, f32[240,128]{1,0:T(8,128)S(1)}, f32[240,128]{1,0:T(8,128)S(1)}, f32[240,128]{1,0:T(8,128)S(1)}, s32[]{:T(128)}, /*index=5*/f32[240,...) while((s32[]{:T(128)}, f32[240,128]{1,0:T(8,128)S(1)}, ...), condition=%wide.region_2.3_spmd.clone, body=%wide.region_0.2_spmd.clone.sunk | while | flops 1133230080 | bytes 11526409 | solution.py:50
  24.1 3.1 convolution_select_fusion.3
  27.2 189.0 %all-reduce.5.cloned.1.call-done = f32[240,1024]{1,0:T(8,128)} async-done(((f32[240,1024]{1,0:T(8,128)}), f32[240,1024]{1,0:T(8,128)}) %all-reduce.5.cloned.1.call-update) | async-done | bytes 983056 | tf_op jit(solution)/shard_map/while/body/eval_jaxpr/psum | solution.py:31
  216.2 2.3 convolution_add_fusion.2
  221.9 3.0 convolution_select_fusion.3
  224.9 187.0 %all-reduce.5.cloned.1.call-done = f32[240,1024]{1,0:T(8,128)} async-done(((f32[240,1024]{1,0:T(8,128)}), f32[240,1024]{1,0:T(8,128)}) %all-reduce.5.cloned.1.call-update) | async-done | bytes 983056 | tf_op jit(solution)/shard_map/while/body/eval_jaxpr/psum | solution.py:31
  411.9 2.3 convolution_add_fusion.2
  414.3 2.3 fusion.32
  417.6 3.0 convolution_select_fusion.3
  420.7 187.0 %all-reduce.5.cloned.1.call-done = f32[240,1024]{1,0:T(8,128)} async-done(((f32[240,1024]{1,0:T(8,128)}), f32[240,1024]{1,0:T(8,128)}) %all-reduce.5.cloned.1.call-update) | async-done | bytes 983056 | tf_op jit(solution)/shard_map/while/body/eval_jaxpr/psum | solution.py:31
  607.7 2.3 convolution_add_fusion.2
  610.0 2.3 fusion.32
  613.3 3.0 convolution_select_fusion.3
  616.4 186.7 %all-reduce.5.cloned.1.call-done = f32[240,1024]{1,0:T(8,128)} async-done(((f32[240,1024]{1,0:T(8,128)}), f32[240,1024]{1,0:T(8,128)}) %all-reduce.5.cloned.1.call-update) | async-done | bytes 983056 | tf_op jit(solution)/shard_map/while/body/eval_jaxpr/psum | solution.py:31
  803.1 2.3 convolution_add_fusion.2
  808.7 3.0 convolution_select_fusion.3
  811.8 186.7 %all-reduce.5.cloned.1.call-done = f32[240,1024]{1,0:T(8,128)} async-done(((f32[240,1024]{1,0:T(8,128)}), f32[240,1024]{1,0:T(8,128)}) %all-reduce.5.cloned.1.call-update) | async-done | bytes 983056 | tf_op jit(solution)/shard_map/while/body/eval_jaxpr/psum | solution.py:31
  998.5 2.3 convolution_add_fusion.2
  1004.2 3.0 convolution_select_fusion.3
  1007.2 187.4 %all-reduce.5.cloned.1.call-done = f32[240,1024]{1,0:T(8,128)} async-done(((f32[240,1024]{1,0:T(8,128)}), f32[240,1024]{1,0:T(8,128)}) %all-reduce.5.cloned.1.call-update) | async-done | bytes 983056 | tf_op jit(solution)/shard_map/while/body/eval_jaxpr/psum | solution.py:31
  1194.6 2.3 convolution_add_fusion.2
  1200.3 3.0 convolution_select_fusion.3
  1203.4 187.4 %all-reduce.5.cloned.1.call-done = f32[240,1024]{1,0:T(8,128)} async-done(((f32[240,1024]{1,0:T(8,128)}), f32[240,1024]{1,0:T(8,128)}) %all-reduce.5.cloned.1.call-update) | async-done | bytes 983056 | tf_op jit(solution)/shard_map/while/body/eval_jaxpr/psum | solution.py:31
  1390.8 2.3 convolution_add_fusion.2
  1393.2 2.3 fusion.32
  1396.5 3.0 convolution_select_fusion.3
  1399.6 187.0 %all-reduce.5.cloned.1.call-done = f32[240,1024]{1,0:T(8,128)} async-done(((f32[240,1024]{1,0:T(8,128)}), f32[240,1024]{1,0:T(8,128)}) %all-reduce.5.cloned.1.call-update) | async-done | bytes 983056 | tf_op jit(solution)/shard_map/while/body/eval_jaxpr/psum | solution.py:31
  1586.6 2.3 convolution_add_fusion.2
  1593.3 8.3 all-to-all-start
  1603.0 11.3 all-to-all-done
  1615.6 43.0 %all-reduce.3.cloned.1.call-done = f32[240,256]{1,0:T(8,128)} async-done(((f32[240,256]{1,0:T(8,128)}), f32[240,256]{1,0:T(8,128)}) %all-reduce.3.cloned.1.call-update) | async-done | bytes 245776 | tf_op jit(solution)/shard_map/psum | solution.py:93
  (55 shorter events, 28.9 us)
Async XLA Ops:
  11.9 1581.4 %all-to-all-start.1 = ((s32[64,1,4]{2,1,0:T(1,128)}), s32[64,1,4]{2,1,0:T(1,128)S(1)}, u32[]{:S(2)}, u32[]{:S(2)}) async-start(s32[64,1,4]{2,1,0:T(1,128)} %bitcast.8), calls=%async_computation.1 | async-start | bytes 65536 | tf_op jit(solution)/shard_map/all_to_all | solution.py:76
  24.0 1568.2 %copy-start.2 = (f32[1,240,128]{2,1,0:T(8,128)S(1)}, f32[1,240,128]{2,1,0:T(8,128)}, u32[]{:S(2)}) copy-start(f32[1,240,128]{2,1,0:T(8,128)} %param.14) | copy-start | bytes 368644
  24.0 1634.6 %copy-start.1 = (f32[240,256]{1,0:T(8,128)S(1)}, f32[240,256]{1,0:T(8,128)}, u32[]{:S(2)}) copy-start(f32[240,256]{1,0:T(8,128)} %param.17) | copy-start | bytes 737284
  24.0 192.2 %all-reduce.5.cloned.1.call-start = ((), (), s32[]{:S(2)}) async-start(), calls=%async_computation.3 | async-start | bytes 1966080 | tf_op jit(solution)/shard_map/while/body/eval_jaxpr/psum | solution.py:31
  221.8 190.1 %all-reduce.5.cloned.1.call-start = ((), (), s32[]{:S(2)}) async-start(), calls=%async_computation.3 | async-start | bytes 1966080 | tf_op jit(solution)/shard_map/while/body/eval_jaxpr/psum | solution.py:31
  417.6 190.1 %all-reduce.5.cloned.1.call-start = ((), (), s32[]{:S(2)}) async-start(), calls=%async_computation.3 | async-start | bytes 1966080 | tf_op jit(solution)/shard_map/while/body/eval_jaxpr/psum | solution.py:31
  613.3 189.8 %all-reduce.5.cloned.1.call-start = ((), (), s32[]{:S(2)}) async-start(), calls=%async_computation.3 | async-start | bytes 1966080 | tf_op jit(solution)/shard_map/while/body/eval_jaxpr/psum | solution.py:31
  808.7 189.8 %all-reduce.5.cloned.1.call-start = ((), (), s32[]{:S(2)}) async-start(), calls=%async_computation.3 | async-start | bytes 1966080 | tf_op jit(solution)/shard_map/while/body/eval_jaxpr/psum | solution.py:31
  1004.1 190.5 %all-reduce.5.cloned.1.call-start = ((), (), s32[]{:S(2)}) async-start(), calls=%async_computation.3 | async-start | bytes 1966080 | tf_op jit(solution)/shard_map/while/body/eval_jaxpr/psum | solution.py:31
  1200.3 190.6 %all-reduce.5.cloned.1.call-start = ((), (), s32[]{:S(2)}) async-start(), calls=%async_computation.3 | async-start | bytes 1966080 | tf_op jit(solution)/shard_map/while/body/eval_jaxpr/psum | solution.py:31
  1396.4 190.2 %all-reduce.5.cloned.1.call-start = ((), (), s32[]{:S(2)}) async-start(), calls=%async_computation.3 | async-start | bytes 1966080 | tf_op jit(solution)/shard_map/while/body/eval_jaxpr/psum | solution.py:31
  1592.2 68.1 %copy-start = (f32[240,128]{1,0:T(8,128)}, f32[240,128]{1,0:T(8,128)S(1)}, u32[]{:S(2)}) copy-start(f32[240,128]{1,0:T(8,128)S(1)} %get-tuple-element.239) | copy-start | bytes 368644
  1593.3 21.0 %all-to-all-start = ((f32[64,4,240]{2,1,0:T(4,128)}), f32[64,4,240]{2,1,0:T(4,128)S(1)}, u32[]{:S(2)}, u32[]{:S(2)}) async-start(f32[64,4,240]{2,1,0:T(4,128)} %reshape.25), calls=%async_computation | async-start | bytes 524288 | tf_op jit(solution)/shard_map/all_to_all | solution.py:69
  1601.6 56.9 %all-reduce.3.cloned.1.call-start = ((), (), s32[]{:S(2)}) async-start(), calls=%async_computation.2 | async-start | bytes 491520 | tf_op jit(solution)/shard_map/psum | solution.py:93
Sparse Core Ops, SparseCore 0:
  28.2 187.9 all-reduce.4
  226.0 185.8 all-reduce.4
  421.7 185.8 all-reduce.4
  617.2 185.8 all-reduce.4
  812.6 185.8 all-reduce.4
  1008.0 186.6 all-reduce.4
  1204.5 186.3 all-reduce.4
  1400.6 185.9 all-reduce.4
Sparse Core Ops, SparseCore 1:
  1615.7 42.8 all-reduce.2
where the time goes:
time: 1670 us
  waiting for transfers between devices  1550 us (93%)
  matrix products  62.8 us (4%)
  starting transfers between devices  20.7 us (1%)
    psum x8, waiting for transfers between devices, solve_section(): solved = lax.psum(masked, ('pivot', 'rows'))  1500 us
    psum x1, waiting for transfers between devices, shards(): sibling_total = lax.psum(local_part, 'front')  43 us
  transfers between devices with their start and end apart: 11, of which 10 were waited for; matrix products, arithmetic and copies ran while one was open for 4% of the time, Pallas kernels for 0%

commit v1 on v0

--- a/solution.py
+++ b/solution.py
@@ -4,6 +4,11 @@
 from jax.sharding import PartitionSpec as P
 
 highest = lax.Precision.HIGHEST
+
+
+def by_each_axis(x, inner_axis, outer_axis):
+    partial = lax.psum(x, inner_axis)
+    return lax.psum(partial, outer_axis)
 
 
 def shards(factor, inv_diag, boundary, rhs, boundary_rhs, owner, slot, parent_in):
@@ -28,7 +33,7 @@
             residual, inv_rows, precision=highest, preferred_element_type=jnp.float32
         )
         masked = jnp.where(own_block == section_idx, partial_value, 0.0)
-        solved = lax.psum(masked, ("pivot", "rows"))
+        solved = by_each_axis(masked, "pivot", "rows")
         pivot_tile = lax.dynamic_slice_in_dim(factor_rows, section_idx * block_span, block_span, 1)
         update_term = lax.dot_general(
             solved, pivot_tile, contract, precision=highest, preferred_element_type=jnp.float32

time: 1670 us -> 1320 us (0.79)
  waiting for transfers between devices: 1550 us -> 1200 us
    psum x8 -> x16, waiting for transfers between devices: 1500 us -> 1150 us  [the longest x8 635 us: by_each_axis(): return lax.psum(partial, outer_axis)]
  transfers between devices with their start and end apart: 11 -> 19, of which waited for: 10 -> 18; matrix products, arithmetic and copies ran while one was open for 4% -> 5% of each run, Pallas kernels for 0% -> 0%
where the time goes in v1:
time: 1320 us
  waiting for transfers between devices  1200 us (91%)
  matrix products  62.8 us (5%)
  starting transfers between devices  20.4 us (2%)
  between operations  15.3 us (1%)
    psum x8, waiting for transfers between devices, by_each_axis(): return lax.psum(partial, outer_axis)  635 us
    psum x8, waiting for transfers between devices, by_each_axis(): partial = lax.psum(x, inner_axis)  513 us
    psum x1, waiting for transfers between devices, shards(): sibling_total = lax.psum(local_part, 'front')  43 us
  transfers between devices with their start and end apart: 19, of which 18 were waited for; matrix products, arithmetic and copies ran while one was open for 5% of the time, Pallas kernels for 0%

profile of v1, /device:TPU:2, one launch (start us, length us, event | category | flops | bytes accessed | tf_op | source)
XLA Modules:
  0.0 1317.1 jit_solution(11716667460887189944)
XLA Ops:
  11.9 12.0 all-to-all-start.1
  24.0 1218.5 %while.20 = (s32[]{:T(128)}, f32[240,128]{1,0:T(8,128)S(1)}, f32[240,128]{1,0:T(8,128)S(1)}, f32[240,128]{1,0:T(8,128)S(1)}, s32[]{:T(128)}, /*index=5*/f32[240,...) while((s32[]{:T(128)}, f32[240,128]{1,0:T(8,128)S(1)}, ...), condition=%wide.region_3.4_spmd.clone, body=%wide.region_0.3_spmd.clone.sunk | while | flops 1133475840 | bytes 17424688 | solution.py:55
  24.1 3.1 convolution_select_fusion.3
  27.2 66.6 %all-reduce.6.cloned.1.call-done = f32[240,1024]{1,0:T(8,128)} async-done(((f32[240,1024]{1,0:T(8,128)}), f32[240,1024]{1,0:T(8,128)}) %all-reduce.6.cloned.1.call-update) | async-done | bytes 983056 | tf_op jit(solution)/shard_map/while/body/eval_jaxpr/psum | solution.py:10
  93.9 79.5 %all-reduce.8.cloned.1.call-done = f32[240,1024]{1,0:T(8,128)} async-done(((f32[240,1024]{1,0:T(8,128)}), f32[240,1024]{1,0:T(8,128)}) %all-reduce.8.cloned.1.call-update) | async-done | bytes 983056 | tf_op jit(solution)/shard_map/while/body/eval_jaxpr/psum | solution.py:11
  179.1 3.0 convolution_select_fusion.3
  182.2 63.7 %all-reduce.6.cloned.1.call-done = f32[240,1024]{1,0:T(8,128)} async-done(((f32[240,1024]{1,0:T(8,128)}), f32[240,1024]{1,0:T(8,128)}) %all-reduce.6.cloned.1.call-update) | async-done | bytes 983056 | tf_op jit(solution)/shard_map/while/body/eval_jaxpr/psum | solution.py:10
  246.0 79.4 %all-reduce.8.cloned.1.call-done = f32[240,1024]{1,0:T(8,128)} async-done(((f32[240,1024]{1,0:T(8,128)}), f32[240,1024]{1,0:T(8,128)}) %all-reduce.8.cloned.1.call-update) | async-done | bytes 983056 | tf_op jit(solution)/shard_map/while/body/eval_jaxpr/psum | solution.py:11
  325.3 2.3 convolution_add_fusion.2
  331.0 3.0 convolution_select_fusion.3
  334.1 63.7 %all-reduce.6.cloned.1.call-done = f32[240,1024]{1,0:T(8,128)} async-done(((f32[240,1024]{1,0:T(8,128)}), f32[240,1024]{1,0:T(8,128)}) %all-reduce.6.cloned.1.call-update) | async-done | bytes 983056 | tf_op jit(solution)/shard_map/while/body/eval_jaxpr/psum | solution.py:10
  397.8 79.4 %all-reduce.8.cloned.1.call-done = f32[240,1024]{1,0:T(8,128)} async-done(((f32[240,1024]{1,0:T(8,128)}), f32[240,1024]{1,0:T(8,128)}) %all-reduce.8.cloned.1.call-update) | async-done | bytes 983056 | tf_op jit(solution)/shard_map/while/body/eval_jaxpr/psum | solution.py:11
  482.9 3.0 convolution_select_fusion.3
  486.0 63.7 %all-reduce.6.cloned.1.call-done = f32[240,1024]{1,0:T(8,128)} async-done(((f32[240,1024]{1,0:T(8,128)}), f32[240,1024]{1,0:T(8,128)}) %all-reduce.6.cloned.1.call-update) | async-done | bytes 983056 | tf_op jit(solution)/shard_map/while/body/eval_jaxpr/psum | solution.py:10
  549.7 79.5 %all-reduce.8.cloned.1.call-done = f32[240,1024]{1,0:T(8,128)} async-done(((f32[240,1024]{1,0:T(8,128)}), f32[240,1024]{1,0:T(8,128)}) %all-reduce.8.cloned.1.call-update) | async-done | bytes 983056 | tf_op jit(solution)/shard_map/while/body/eval_jaxpr/psum | solution.py:11
  634.9 3.0 convolution_select_fusion.3
  638.0 63.7 %all-reduce.6.cloned.1.call-done = f32[240,1024]{1,0:T(8,128)} async-done(((f32[240,1024]{1,0:T(8,128)}), f32[240,1024]{1,0:T(8,128)}) %all-reduce.6.cloned.1.call-update) | async-done | bytes 983056 | tf_op jit(solution)/shard_map/while/body/eval_jaxpr/psum | solution.py:10
  701.8 79.3 %all-reduce.8.cloned.1.call-done = f32[240,1024]{1,0:T(8,128)} async-done(((f32[240,1024]{1,0:T(8,128)}), f32[240,1024]{1,0:T(8,128)}) %all-reduce.8.cloned.1.call-update) | async-done | bytes 983056 | tf_op jit(solution)/shard_map/while/body/eval_jaxpr/psum | solution.py:11
  786.8 3.0 convolution_select_fusion.3
  789.9 63.7 %all-reduce.6.cloned.1.call-done = f32[240,1024]{1,0:T(8,128)} async-done(((f32[240,1024]{1,0:T(8,128)}), f32[240,1024]{1,0:T(8,128)}) %all-reduce.6.cloned.1.call-update) | async-done | bytes 983056 | tf_op jit(solution)/shard_map/while/body/eval_jaxpr/psum | solution.py:10
  853.7 79.4 %all-reduce.8.cloned.1.call-done = f32[240,1024]{1,0:T(8,128)} async-done(((f32[240,1024]{1,0:T(8,128)}), f32[240,1024]{1,0:T(8,128)}) %all-reduce.8.cloned.1.call-update) | async-done | bytes 983056 | tf_op jit(solution)/shard_map/while/body/eval_jaxpr/psum | solution.py:11
  933.0 2.3 convolution_add_fusion.2
  938.7 3.0 convolution_select_fusion.3
  941.8 63.7 %all-reduce.6.cloned.1.call-done = f32[240,1024]{1,0:T(8,128)} async-done(((f32[240,1024]{1,0:T(8,128)}), f32[240,1024]{1,0:T(8,128)}) %all-reduce.6.cloned.1.call-update) | async-done | bytes 983056 | tf_op jit(solution)/shard_map/while/body/eval_jaxpr/psum | solution.py:10
  1005.6 79.4 %all-reduce.8.cloned.1.call-done = f32[240,1024]{1,0:T(8,128)} async-done(((f32[240,1024]{1,0:T(8,128)}), f32[240,1024]{1,0:T(8,128)}) %all-reduce.8.cloned.1.call-update) | async-done | bytes 983056 | tf_op jit(solution)/shard_map/while/body/eval_jaxpr/psum | solution.py:11
  1090.6 3.0 convolution_select_fusion.3
  1093.7 63.7 %all-reduce.6.cloned.1.call-done = f32[240,1024]{1,0:T(8,128)} async-done(((f32[240,1024]{1,0:T(8,128)}), f32[240,1024]{1,0:T(8,128)}) %all-reduce.6.cloned.1.call-update) | async-done | bytes 983056 | tf_op jit(solution)/shard_map/while/body/eval_jaxpr/psum | solution.py:10
  1157.5 79.4 %all-reduce.8.cloned.1.call-done = f32[240,1024]{1,0:T(8,128)} async-done(((f32[240,1024]{1,0:T(8,128)}), f32[240,1024]{1,0:T(8,128)}) %all-reduce.8.cloned.1.call-update) | async-done | bytes 983056 | tf_op jit(solution)/shard_map/while/body/eval_jaxpr/psum | solution.py:11
  1236.9 2.3 convolution_add_fusion.2
  1243.6 7.7 all-to-all-start
  1252.7 11.3 all-to-all-done
  1265.3 43.0 %all-reduce.4.cloned.1.call-done = f32[240,256]{1,0:T(8,128)} async-done(((f32[240,256]{1,0:T(8,128)}), f32[240,256]{1,0:T(8,128)}) %all-reduce.4.cloned.1.call-update) | async-done | bytes 245776 | tf_op jit(solution)/shard_map/psum | solution.py:98
  (79 shorter events, 47.9 us)
Async XLA Ops:
  11.9 1231.7 %all-to-all-start.1 = ((s32[64,1,4]{2,1,0:T(1,128)}), s32[64,1,4]{2,1,0:T(1,128)S(1)}, u32[]{:S(2)}, u32[]{:S(2)}) async-start(s32[64,1,4]{2,1,0:T(1,128)} %bitcast.8), calls=%async_computation.1 | async-start | bytes 65536 | tf_op jit(solution)/shard_map/all_to_all | solution.py:81
  24.0 1218.6 %copy-start.2 = (f32[1,240,128]{2,1,0:T(8,128)S(1)}, f32[1,240,128]{2,1,0:T(8,128)}, u32[]{:S(2)}) copy-start(f32[1,240,128]{2,1,0:T(8,128)} %param.14) | copy-start | bytes 368644
  24.0 1284.3 %copy-start.1 = (f32[240,256]{1,0:T(8,128)S(1)}, f32[240,256]{1,0:T(8,128)}, u32[]{:S(2)}) copy-start(f32[240,256]{1,0:T(8,128)} %param.17) | copy-start | bytes 737284
  24.0 69.9 %all-reduce.6.cloned.1.call-start = ((), (), s32[]{:S(2)}) async-start(), calls=%async_computation.3 | async-start | bytes 1966080 | tf_op jit(solution)/shard_map/while/body/eval_jaxpr/psum | solution.py:10
  27.2 146.2 %all-reduce.8.cloned.1.call-start = ((), (), s32[]{:S(2)}) async-start(), calls=%async_computation.4 | async-start | bytes 1966080 | tf_op jit(solution)/shard_map/while/body/eval_jaxpr/psum | solution.py:11
  179.0 66.9 %all-reduce.6.cloned.1.call-start = ((), (), s32[]{:S(2)}) async-start(), calls=%async_computation.3 | async-start | bytes 1966080 | tf_op jit(solution)/shard_map/while/body/eval_jaxpr/psum | solution.py:10
  182.1 143.2 %all-reduce.8.cloned.1.call-start = ((), (), s32[]{:S(2)}) async-start(), calls=%async_computation.4 | async-start | bytes 1966080 | tf_op jit(solution)/shard_map/while/body/eval_jaxpr/psum | solution.py:11
  330.9 66.9 %all-reduce.6.cloned.1.call-start = ((), (), s32[]{:S(2)}) async-start(), calls=%async_computation.3 | async-start | bytes 1966080 | tf_op jit(solution)/shard_map/while/body/eval_jaxpr/psum | solution.py:10
  334.0 143.2 %all-reduce.8.cloned.1.call-start = ((), (), s32[]{:S(2)}) async-start(), calls=%async_computation.4 | async-start | bytes 1966080 | tf_op jit(solution)/shard_map/while/body/eval_jaxpr/psum | solution.py:11
  482.8 66.9 %all-reduce.6.cloned.1.call-start = ((), (), s32[]{:S(2)}) async-start(), calls=%async_computation.3 | async-start | bytes 1966080 | tf_op jit(solution)/shard_map/while/body/eval_jaxpr/psum | solution.py:10
  485.9 143.3 %all-reduce.8.cloned.1.call-start = ((), (), s32[]{:S(2)}) async-start(), calls=%async_computation.4 | async-start | bytes 1966080 | tf_op jit(solution)/shard_map/while/body/eval_jaxpr/psum | solution.py:11
  634.9 66.9 %all-reduce.6.cloned.1.call-start = ((), (), s32[]{:S(2)}) async-start(), calls=%async_computation.3 | async-start | bytes 1966080 | tf_op jit(solution)/shard_map/while/body/eval_jaxpr/psum | solution.py:10
  638.0 143.2 %all-reduce.8.cloned.1.call-start = ((), (), s32[]{:S(2)}) async-start(), calls=%async_computation.4 | async-start | bytes 1966080 | tf_op jit(solution)/shard_map/while/body/eval_jaxpr/psum | solution.py:11
  786.7 66.9 %all-reduce.6.cloned.1.call-start = ((), (), s32[]{:S(2)}) async-start(), calls=%async_computation.3 | async-start | bytes 1966080 | tf_op jit(solution)/shard_map/while/body/eval_jaxpr/psum | solution.py:10
  789.9 143.2 %all-reduce.8.cloned.1.call-start = ((), (), s32[]{:S(2)}) async-start(), calls=%async_computation.4 | async-start | bytes 1966080 | tf_op jit(solution)/shard_map/while/body/eval_jaxpr/psum | solution.py:11
  938.6 66.9 %all-reduce.6.cloned.1.call-start = ((), (), s32[]{:S(2)}) async-start(), calls=%async_computation.3 | async-start | bytes 1966080 | tf_op jit(solution)/shard_map/while/body/eval_jaxpr/psum | solution.py:10
  941.8 143.2 %all-reduce.8.cloned.1.call-start = ((), (), s32[]{:S(2)}) async-start(), calls=%async_computation.4 | async-start | bytes 1966080 | tf_op jit(solution)/shard_map/while/body/eval_jaxpr/psum | solution.py:11
  1090.5 66.9 %all-reduce.6.cloned.1.call-start = ((), (), s32[]{:S(2)}) async-start(), calls=%async_computation.3 | async-start | bytes 1966080 | tf_op jit(solution)/shard_map/while/body/eval_jaxpr/psum | solution.py:10
  1093.7 143.3 %all-reduce.8.cloned.1.call-start = ((), (), s32[]{:S(2)}) async-start(), calls=%async_computation.4 | async-start | bytes 1966080 | tf_op jit(solution)/shard_map/while/body/eval_jaxpr/psum | solution.py:11
  1242.5 67.5 %copy-start = (f32[240,128]{1,0:T(8,128)}, f32[240,128]{1,0:T(8,128)S(1)}, u32[]{:S(2)}) copy-start(f32[240,128]{1,0:T(8,128)S(1)} %get-tuple-element.239) | copy-start | bytes 368644
  1243.6 20.4 %all-to-all-start = ((f32[64,4,240]{2,1,0:T(4,128)}), f32[64,4,240]{2,1,0:T(4,128)S(1)}, u32[]{:S(2)}, u32[]{:S(2)}) async-start(f32[64,4,240]{2,1,0:T(4,128)} %reshape.25), calls=%async_computation | async-start | bytes 524288 | tf_op jit(solution)/shard_map/all_to_all | solution.py:74
  1251.3 56.9 %all-reduce.4.cloned.1.call-start = ((), (), s32[]{:S(2)}) async-start(), calls=%async_computation.2 | async-start | bytes 491520 | tf_op jit(solution)/shard_map/psum | solution.py:98
Sparse Core Ops, SparseCore 0:
  27.3 66.5 all-reduce.5
  96.2 77.1 all-reduce.7
  182.2 63.6 all-reduce.5
  248.1 77.1 all-reduce.7
  334.1 63.6 all-reduce.5
  400.0 77.1 all-reduce.7
  486.0 63.6 all-reduce.5
  552.1 77.1 all-reduce.7
  638.1 63.6 all-reduce.5
  704.0 77.1 all-reduce.7
  790.0 63.6 all-reduce.5
  855.9 77.1 all-reduce.7
  941.9 63.6 all-reduce.5
  1007.8 77.1 all-reduce.7
  1093.8 63.6 all-reduce.5
  1159.7 77.2 all-reduce.7
Sparse Core Ops, SparseCore 1:
  1265.4 42.9 all-reduce.3
